TPU v7x, 32 devices: a whole 2x2x4 slice. The times are simulated.
32 devices in a mesh: dp: 4 (over y, x), mp: 8 (over z, core).
Axes of the slice: x: 2, y: 2, z: 4, core: 2. Of those that a mesh axis runs over, the one named last changes fastest.
Arguments:
- tokens: bfloat16 [4096, 2048], P(('dp', 'mp')), may hold values from -9 to 9
- seg_ids: int32 [4096], P('dp'), may hold values from 0 to 12, as said below
- positions: int32 [4096], P('dp'), may hold values from 0 to 1023, as said below
- w_query: bfloat16 [2048, 2048], P(None, 'mp'), may hold values from -0.125 to 0.125
- w_key: bfloat16 [2048, 512], replicated, may hold values from -0.125 to 0.125
- w_value: bfloat16 [2048, 512], replicated, may hold values from -0.125 to 0.125
- w_output: bfloat16 [2048, 2048], P('mp'), may hold values from -0.75 to 0.75
- w_gate: bfloat16 [2048, 8192], P(None, 'mp'), may hold values from -0.125 to 0.125
- w_up: bfloat16 [2048, 8192], P(None, 'mp'), may hold values from -0.125 to 0.125
- w_down: bfloat16 [8192, 2048], P('mp'), may hold values from -0.0625 to 0.0625
- attn_gain: float32 [2048], replicated, may hold values from 0.5 to 1.5
- ffn_gain: float32 [2048], replicated, may hold values from 0.5 to 1.5
- query_gain: float32 [64], replicated, may hold values from 0.1 to 1.9
- key_gain: float32 [64], replicated, may hold values from 0.1 to 1.9
- out_grad: bfloat16 [4096, 2048], P(('dp', 'mp')), may hold values from -6 to 6
Outputs:
- output: bfloat16 [4096, 2048], P(('dp', 'mp'))
- grad_tokens: bfloat16 [4096, 2048], P(('dp', 'mp'))
- grad_w_query: float32 [2048, 2048], P(None, 'mp')
- grad_w_key: float32 [2048, 512], replicated
- grad_w_value: float32 [2048, 512], replicated
- grad_w_output: float32 [2048, 2048], P('mp')
- grad_w_gate: float32 [2048, 8192], P(None, 'mp')
- grad_w_up: float32 [2048, 8192], P(None, 'mp')
- grad_w_down: float32 [8192, 2048], P('mp')
- grad_attn_gain: float32 [2048], replicated
- grad_ffn_gain: float32 [2048], replicated
- grad_query_gain: float32 [64], replicated
- grad_key_gain: float32 [64], replicated
- residual_rms: float32 [1], replicated
- branch_rms: float32 [2, 4096], P(None, ('dp', 'mp'))
Inputs may be any that keep to these rules, and one draw needn't show every extreme that they name: `seg_ids`: never falling along the tokens; the first token of every block of 1024 consecutive tokens starts a new segment; the first block is one segment, every other block holds exactly 4. `positions`: 0 at the first token of a segment, one more at each following token of it.
All inputs are finite; a program needn't handle non-finite values.
Results may differ from a plain program's by a relative error of at most 0.015.
Values may be sent and summed in bfloat16 or wider, within the bound.
A program may use at most 256 MiB of HBM per device.

v0:
```python
import jax
import jax.numpy as jnp
from jax import lax
from jax.sharding import PartitionSpec as P

HEADS = 32
KV = 8
HD = 64
EPSILON = 1e-06
ROPE_BASE = 10000.0
MASKED = -1e30


def matmul(left, right):
    return jnp.dot(left, right, preferred_element_type=jnp.float32)


def matmul_left_t(left, right):
    return lax.dot_general(
        left, right, (((0,), (0,)), ((), ())), preferred_element_type=jnp.float32
    )


def matmul_right_t(left, right):
    return lax.dot_general(
        left, right, (((1,), (1,)), ((), ())), preferred_element_type=jnp.float32
    )


def rope_tables(position_row):
    half = HD // 2
    freq = ROPE_BASE ** (-jnp.arange(half, dtype=jnp.float32) / half)
    angle = position_row.astype(jnp.float32)[:, None] * freq[None, :]
    return (jnp.cos(angle)[:, None, :], jnp.sin(angle)[:, None, :])


def rotate(values, cosine, sine):
    half = HD // 2
    first_half = values[..., :half]
    second_half = values[..., half:]
    return jnp.concatenate(
        [first_half * cosine - second_half * sine, second_half * cosine + first_half * sine], -1
    )


def unrotate(grads, cosine, sine):
    half = HD // 2
    first_half = grads[..., :half]
    second_half = grads[..., half:]
    return jnp.concatenate(
        [first_half * cosine + second_half * sine, second_half * cosine - first_half * sine], -1
    )


def norm_back(grad_normed, unit, inverse, gain):
    scaled = grad_normed * gain
    return inverse * (scaled - unit * jnp.mean(scaled * unit, -1, keepdims=True))


def per_device(
    tokens,
    seg_ids,
    positions,
    w_query,
    w_key,
    w_value,
    w_output,
    w_gate,
    w_up,
    w_down,
    attn_gain,
    ffn_gain,
    query_gain,
    key_gain,
    out_grad,
):
    tok_count = tokens.shape[0]
    model_width = tokens.shape[1]
    row_count = tok_count * lax.axis_size("mp")
    query_width = w_query.shape[1]
    heads_dev = query_width // HD
    ffn_width = w_gate.shape[1]
    group = lax.axis_index("mp") * heads_dev // (HEADS // KV)
    score_scale = HD ** (-0.5)
    tokens_f = tokens.astype(jnp.float32)
    inv_one = lax.rsqrt(jnp.mean(tokens_f * tokens_f, -1, keepdims=True) + EPSILON)
    normed_one = tokens_f * inv_one
    h_one = (normed_one * attn_gain).astype(jnp.bfloat16)
    key_cols = lax.dynamic_slice_in_dim(w_key, group * HD, HD, 1)
    value_cols = lax.dynamic_slice_in_dim(w_value, group * HD, HD, 1)
    w_attn = jnp.concatenate([w_query, key_cols, value_cols], 1)
    gathered_one = lax.all_gather(h_one, "mp", axis=0, tiled=True)
    projected = matmul(gathered_one, w_attn)
    query = projected[:, :query_width].reshape(row_count, heads_dev, HD)
    key_proj = projected[:, query_width : query_width + HD]
    value_low = projected[:, query_width + HD :].astype(jnp.bfloat16)
    query_inv = lax.rsqrt(jnp.mean(query * query, -1, keepdims=True) + EPSILON)
    query_unit = query * query_inv
    key_inv = lax.rsqrt(jnp.mean(key_proj * key_proj, -1, keepdims=True) + EPSILON)
    key_unit = key_proj * key_inv
    cosine, sine = rope_tables(positions)
    query_rot = rotate(query_unit * query_gain, cosine, sine).astype(jnp.bfloat16)
    key_rot = rotate((key_unit * key_gain)[:, None, :], cosine, sine)[:, 0, :].astype(jnp.bfloat16)
    block = min(512, row_count)
    block_count = row_count // block
    token_index = jnp.arange(row_count, dtype=jnp.int32)
    starts = jnp.arange(block_count, dtype=jnp.int32) * block
    query_blocks = query_rot.reshape(block_count, block, heads_dev, HD)

    def block_scores(query_block, start):
        scores = (
            jnp.einsum("qhd,kd->hqk", query_block, key_rot, preferred_element_type=jnp.float32)
            * score_scale
        )
        segment_block = lax.dynamic_slice_in_dim(seg_ids, start, block)
        index_block = start + jnp.arange(block, dtype=jnp.int32)
        allowed = (segment_block[:, None] == seg_ids[None, :]) & (
            token_index[None, :] <= index_block[:, None]
        )
        return jnp.where(allowed[None], scores, MASKED)

    def forward_block(inputs):
        query_block, start = inputs
        scores = block_scores(query_block, start)
        top = jnp.max(scores, -1, keepdims=True)
        expo = jnp.exp(scores - top)
        total = jnp.sum(expo, -1, keepdims=True)
        probs = (expo / total).astype(jnp.bfloat16)
        context_block = jnp.einsum(
            "hqk,kd->qhd", probs, value_low, preferred_element_type=jnp.float32
        )
        return (context_block.astype(jnp.bfloat16), (top + jnp.log(total))[..., 0])

    context_blocks, lse_blocks = lax.map(forward_block, (query_blocks, starts))
    context = context_blocks.reshape(row_count, query_width)
    attn_branch = lax.psum_scatter(matmul(context, w_output), "mp", scatter_dimension=0, tiled=True)
    residual_mid = tokens_f + attn_branch
    inv_two = lax.rsqrt(jnp.mean(residual_mid * residual_mid, -1, keepdims=True) + EPSILON)
    normed_two = residual_mid * inv_two
    h_two = (normed_two * ffn_gain).astype(jnp.bfloat16)
    w_ffn = jnp.concatenate([w_gate, w_up], 1)
    gathered_two = lax.all_gather(h_two, "mp", axis=0, tiled=True)
    gate_up = matmul(gathered_two, w_ffn)
    gate = gate_up[:, :ffn_width]
    up = gate_up[:, ffn_width:]
    sigma = jax.nn.sigmoid(gate)
    silu_gate = gate * sigma
    hidden = (silu_gate * up).astype(jnp.bfloat16)
    ffn_branch = lax.psum_scatter(
        matmul(hidden, w_down).astype(jnp.bfloat16), "mp", scatter_dimension=0, tiled=True
    ).astype(jnp.float32)
    output = (residual_mid + ffn_branch).astype(jnp.bfloat16)
    branch_rms = jnp.stack(
        [
            jnp.sqrt(jnp.mean(attn_branch * attn_branch, -1)),
            jnp.sqrt(jnp.mean(ffn_branch * ffn_branch, -1)),
        ]
    )
    squares_local = jnp.sum(tokens_f * tokens_f)
    squares_total = lax.psum(squares_local, ("dp", "mp"))
    grad_out = out_grad.astype(jnp.float32)
    grad_ffn_rows = lax.all_gather(out_grad, "mp", axis=0, tiled=True)
    grad_hidden = matmul_right_t(grad_ffn_rows, w_down)
    grad_w_down = matmul_left_t(hidden, grad_ffn_rows)
    grad_gate = grad_hidden * up * sigma * (1.0 + gate * (1.0 - sigma))
    grad_up = grad_hidden * silu_gate
    grad_gate_up = jnp.concatenate([grad_gate, grad_up], 1).astype(jnp.bfloat16)
    grad_w_ffn = matmul_left_t(gathered_two, grad_gate_up)
    grad_h_two = lax.psum_scatter(
        matmul_right_t(grad_gate_up, w_ffn), "mp", scatter_dimension=0, tiled=True
    )
    grad_ffn_gain = jnp.sum(grad_h_two * normed_two, 0)
    grad_mid = grad_out + norm_back(grad_h_two, normed_two, inv_two, ffn_gain)
    grad_attn_rows = lax.all_gather(grad_mid.astype(jnp.bfloat16), "mp", axis=0, tiled=True)
    grad_w_output = matmul_left_t(context, grad_attn_rows)
    grad_context = matmul_right_t(grad_attn_rows, w_output).astype(jnp.bfloat16)
    grad_context_blocks = grad_context.reshape(block_count, block, heads_dev, HD)

    def backward_block(carry, inputs):
        grad_key_acc, grad_value_acc = carry
        query_block, grad_block, lse_block, start = inputs
        scores = block_scores(query_block, start)
        exact = jnp.exp(scores - lse_block[..., None])
        grad_probs = jnp.einsum(
            "qhd,kd->hqk", grad_block, value_low, preferred_element_type=jnp.float32
        )
        delta = jnp.sum(exact * grad_probs, -1, keepdims=True)
        grad_scores = (exact * (grad_probs - delta)).astype(jnp.bfloat16)
        grad_query_block = (
            jnp.einsum("hqk,kd->qhd", grad_scores, key_rot, preferred_element_type=jnp.float32)
            * score_scale
        )
        grad_key_acc = (
            grad_key_acc
            + jnp.einsum(
                "hqk,qhd->kd", grad_scores, query_block, preferred_element_type=jnp.float32
            )
            * score_scale
        )
        grad_value_acc = grad_value_acc + jnp.einsum(
            "hqk,qhd->kd",
            exact.astype(jnp.bfloat16),
            grad_block,
            preferred_element_type=jnp.float32,
        )
        return ((grad_key_acc, grad_value_acc), grad_query_block)

    zero_rows = jnp.zeros((row_count, HD), jnp.float32)
    (grad_key_rot, grad_value), grad_query_blocks = lax.scan(
        backward_block,
        (zero_rows, zero_rows),
        (query_blocks, grad_context_blocks, lse_blocks, starts),
    )
    grad_query_rot = grad_query_blocks.reshape(row_count, heads_dev, HD)
    grad_query_normed = unrotate(grad_query_rot, cosine, sine)
    grad_key_normed = unrotate(grad_key_rot[:, None, :], cosine, sine)[:, 0, :]
    grad_query_gain = jnp.sum(grad_query_normed * query_unit, (0, 1))
    grad_key_gain = jnp.sum(grad_key_normed * key_unit, 0)
    grad_query = norm_back(grad_query_normed, query_unit, query_inv, query_gain)
    grad_key = norm_back(grad_key_normed, key_unit, key_inv, key_gain)
    grad_proj = jnp.concatenate(
        [grad_query.reshape(row_count, query_width), grad_key, grad_value], 1
    ).astype(jnp.bfloat16)
    grad_w_attn = matmul_left_t(gathered_one, grad_proj)
    grad_h_one = lax.psum_scatter(
        matmul_right_t(grad_proj, w_attn), "mp", scatter_dimension=0, tiled=True
    )
    grad_attn_gain = jnp.sum(grad_h_one * normed_one, 0)
    grad_tokens = (grad_mid + norm_back(grad_h_one, normed_one, inv_one, attn_gain)).astype(
        jnp.bfloat16
    )
    grad_w_query = grad_w_attn[:, :query_width]
    key_zeros = jnp.zeros(w_key.shape, jnp.float32)
    grad_w_key = lax.dynamic_update_slice_in_dim(
        key_zeros, grad_w_attn[:, query_width : query_width + HD], group * HD, 1
    )
    grad_w_value = lax.dynamic_update_slice_in_dim(
        key_zeros, grad_w_attn[:, query_width + HD :], group * HD, 1
    )
    grad_w_gate = grad_w_ffn[:, :ffn_width]
    grad_w_up = grad_w_ffn[:, ffn_width:]
    summed = lax.psum((grad_w_query, grad_w_output, grad_w_gate, grad_w_up, grad_w_down), "dp")
    shared = lax.psum(
        (grad_w_key, grad_w_value, grad_attn_gain, grad_ffn_gain, grad_query_gain, grad_key_gain),
        ("dp", "mp"),
    )
    entry_count = tok_count * model_width * lax.axis_size("dp") * lax.axis_size("mp")
    residual_rms = jnp.sqrt(squares_total / entry_count).reshape(1)
    return (
        output,
        grad_tokens,
        summed[0],
        shared[0],
        shared[1],
        summed[1],
        summed[2],
        summed[3],
        summed[4],
        shared[2],
        shared[3],
        shared[4],
        shared[5],
        residual_rms,
        branch_rms,
    )


def solution(mesh):
    return jax.shard_map(
        per_device,
        mesh=mesh,
        in_specs=(
            P(("dp", "mp"), None),
            P("dp"),
            P("dp"),
            P(None, "mp"),
            P(),
            P(),
            P("mp", None),
            P(None, "mp"),
            P(None, "mp"),
            P("mp", None),
            P(),
            P(),
            P(),
            P(),
            P(("dp", "mp"), None),
        ),
        out_specs=(
            P(("dp", "mp"), None),
            P(("dp", "mp"), None),
            P(None, "mp"),
            P(),
            P(),
            P("mp", None),
            P(None, "mp"),
            P(None, "mp"),
            P("mp", None),
            P(),
            P(),
            P(),
            P(),
            P(),
            P(None, ("dp", "mp")),
        ),
        check_vma=False,
    )
```

profile of v0, /device:TPU:0, one launch (start us, length us, event | category | flops | bytes accessed | tf_op | source)
XLA Modules:
  0.0 1435.8 jit_solution(14209004250411522282)
XLA Ops:
  15.5 45.7 %all-gather.5.cloned.1.call-done = bf16[1024,2048]{1,0:T(8,128)(2,1)} async-done(((bf16[128,2048]{1,0:T(8,128)(2,1)}), bf16[1024,2048]{1,0:T(8,128)(2,1)}) %all-gather.5.cloned.1.call-update) | async-done | bytes 4194320 | tf_op jit(solution)/shard_map/all_gather | solution.py:92
  61.2 4.5 fusion.78
  70.9 25.0 %while.28 = (s32[]{:T(128)}, bf16[2,512,4,64]{1,3,2,0:T(8,128)(2,1)}, f32[2,4,512]{2,1,0:T(4,128)}, s32[2]{0:T(128)}, s32[1024]{0:T(1024)S(1)}, /*index=5*/bf16[...) while((s32[]{:T(128)}, ...), condition=%wide.region_6.7_spmd.clone, body=%wide.region_3.6_spmd.clone.sunk | while | flops 563739136 | bytes 32454952 | solution.py:134
  79.6 3.1 fusion.148
  92.1 3.1 fusion.148
  97.7 4.7 fusion.102
  102.9 88.0 %reduce-scatter.5.cloned.1.call-done = f32[128,2048]{1,0:T(8,128)} async-done(((f32[1024,2048]{1,0:T(8,128)}), f32[128,2048]{1,0:T(8,128)}) %reduce-scatter.5.cloned.1.call-update) | async-done | bytes 1048592 | tf_op jit(solution)/shard_map/reduce_scatter | solution.py:136
  194.7 4.8 constant_dynamic-update-slice_fusion.1
  202.0 37.7 %all-gather.7.cloned.1.call-done = bf16[1024,2048]{1,0:T(8,128)(2,1)} async-done(((bf16[128,2048]{1,0:T(8,128)(2,1)}), bf16[1024,2048]{1,0:T(8,128)(2,1)}) %all-gather.7.cloned.1.call-update) | async-done | bytes 4194320 | tf_op jit(solution)/shard_map/all_gather | solution.py:142
  239.7 14.5 %fusion.103 = f32[1024,2048]{1,0:T(8,128)} fusion(bf16[1024,2048]{1,0:T(8,128)(2,1)} %all-gather.7.cloned.1.call-done, bf16[2048,2048]{1,0:T(8,128)(2,1)} %constant_dynamic-update-slice_fusion), kind=kOutput, calls=%fused_computation.175 | convolution fusion | flops 8589934592 | bytes 20971520 | tf_op jit(solution)/shard_map/dot_general | solution.py:15
  254.2 33.1 %all-gather.9.cloned.1.call-done = bf16[1024,2048]{1,0:T(8,128)(2,1)} async-done(((bf16[128,2048]{1,0:T(8,128)(2,1)}), bf16[1024,2048]{1,0:T(8,128)(2,1)}) %all-gather.9.cloned.1.call-update) | async-done | bytes 4194320 | tf_op jit(solution)/shard_map/all_gather | solution.py:162
  287.2 13.1 multiply_convert_fusion.1
  302.4 13.3 fusion.58
  315.9 88.1 %reduce-scatter.9.cloned.1.call-done = f32[128,2048]{1,0:T(8,128)} async-done(((f32[1024,2048]{1,0:T(8,128)}), f32[128,2048]{1,0:T(8,128)}) %reduce-scatter.9.cloned.1.call-update) | async-done | bytes 1048592 | tf_op jit(solution)/shard_map/reduce_scatter | solution.py:169
  409.3 44.9 %all-gather.11.cloned.1.call-done = bf16[1024,2048]{1,0:T(8,128)(2,1)} async-done(((bf16[128,2048]{1,0:T(8,128)(2,1)}), bf16[1024,2048]{1,0:T(8,128)(2,1)}) %all-gather.11.cloned.1.call-update) | async-done | bytes 4194320 | tf_op jit(solution)/shard_map/all_gather | solution.py:174
  454.2 3.5 convolution_convert_fusion.1
  459.4 80.9 %while.29 = (s32[]{:T(128)}, f32[1024,64]{0,1:T(8,128)S(1)}, f32[1024,64]{0,1:T(8,128)}, f32[2,512,4,64]{1,0,3,2:T(2,128)}, s32[2]{0:T(128)S(1)}, /*index=5*/s32...) while((s32[]{:T(128)}, f32[1024,64]{0,1:T(8,128)S(1)}, ...), condition=%wide.region_14.15_spmd.clone, body=%wide.region_12.14_spmd.clone.sunk | while | flops 1375664640 | bytes 114825640 | solution.py:209
  459.4 4.7 fusion.157
  468.0 5.7 fusion.159
  474.0 3.7 fusion.160
  477.7 3.1 fusion.161
  480.8 5.9 fusion.162
  489.4 10.4 dynamic_update_slice.30
  499.8 4.7 fusion.157
  508.3 5.7 fusion.159
  514.3 3.7 fusion.160
  518.0 3.1 fusion.161
  521.1 5.9 fusion.162
  529.7 10.4 dynamic_update_slice.30
  549.4 5.8 fusion.77
  555.3 9.3 convolution_convert_fusion
  565.1 10.8 fusion.105
  576.0 11.8 fusion.57
  587.8 6.8 fusion.100
  594.6 4.2 fusion.79
  607.7 5.8 dynamic_update_slice.18
  616.0 5.9 dynamic_update_slice.19
  622.6 21.1 %reduce-scatter.11.cloned.1.call-done = f32[128,2048]{1,0:T(8,128)} async-done(((f32[1024,2048]{1,0:T(8,128)}), f32[128,2048]{1,0:T(8,128)}) %reduce-scatter.11.cloned.1.call-update) | async-done | bytes 1048592 | tf_op jit(solution)/shard_map/reduce_scatter | solution.py:225
  646.0 40.0 %all-reduce = (f32[2048]{0:T(1024)}, f32[2048]{0:T(1024)}, f32[64]{0:T(128)}, f32[64]{0:T(128)}, f32[]{:T(128)}) all-reduce(f32[2048]{0:T(1024)S(1)} %get-tuple-element.286, f32[2048]{0:T(1024)S(1)} %copy-done.44, f32[64]{0:T(128)S(1)} %reduce_sum.172, f32[64]{0:T(128)S(1)} %copy-done.55, ...), channel_id=1, replica_groups=mesh['dp'=4,'mp'=8] {'dp','mp'}, use_global_device_ids=true, to_apply=%region_27.28 | all-reduce | flops 4225 | bytes 33800 | tf_op jit(solution)/shard_map/psum | solution.py:243
  686.7 9.3 reduce-scatter.7.cloned.1.call-done
  696.1 3.0 fusion.72
  699.7 514.7 %all-reduce.8.cloned.1.call-done = (f32[2048,256]{0,1:T(8,128)}, f32[256,2048]{1,0:T(8,128)}, f32[2048,1024]{1,0:T(8,128)}, f32[2048,1024]{1,0:T(8,128)}, f32[1024,2048]{1,0:T(8,128)}) async-done(((f32[2048,256]{0,1:T(8,128)}, f32[256,2048]{1,0:T(8,128)}, f32[2048,1024]{1,0:T(8,128)}, f32[2048,1024]{1,0:T(8,128)}, f32[1024,2048]{1,0:T(8,128)}), (f32[2048,256]{0,1:T(8,128)}, f32[256,2048]{1,0:T(8,128)}, ...) | async-done | bytes 29360144 | tf_op jit(solution)/shard_map/psum | solution.py:242
  1214.4 2.9 copy.57
  1217.2 183.4 %all-reduce.6.cloned.1.call-done = (f32[2048,512]{1,0:T(8,128)}, f32[2048,512]{1,0:T(8,128)}) async-done(((f32[2048,512]{1,0:T(8,128)}, f32[2048,512]{1,0:T(8,128)}), (f32[2048,512]{1,0:T(8,128)}, f32[2048,512]{1,0:T(8,128)})) %all-reduce.6.cloned.1.call-update) | async-done | bytes 8388624 | tf_op jit(solution)/shard_map/psum | solution.py:243
  1400.6 4.8 copy.117
  1409.9 9.1 copy.120
  1419.0 4.3 copy.121
  1424.2 3.4 copy.122
  (276 shorter events, 85.1 us)
Async XLA Ops:
  7.2 90.5 %copy-start = (bf16[256,2048]{1,0:T(8,128)(2,1)S(1)}, bf16[256,2048]{1,0:T(8,128)(2,1)}, u32[]{:S(2)}) copy-start(bf16[256,2048]{1,0:T(8,128)(2,1)} %param.25) | copy-start | bytes 3145732
  7.2 54.0 %all-gather.5.cloned.1.call-start = ((), (), s32[]{:S(2)}) async-start(), calls=%async_computation.4 | async-start | bytes 4718592 | tf_op jit(solution)/shard_map/all_gather | solution.py:92
  11.2 179.7 %reduce-scatter.5.cloned.1.call-start = ((), (), s32[]{:S(2)}) async-start(), calls=%async_computation.5 | async-start | bytes 9437184 | tf_op jit(solution)/shard_map/reduce_scatter | solution.py:136
  12.0 58.3 %copy-start.42 = (f32[1024]{0:T(1024)}, f32[1024]{0:T(1024)S(1)}, u32[]{:S(2)}) copy-start(f32[1024]{0:T(1024)S(1)} %convert_element_type.62) | copy-start | bytes 12292
  12.5 57.8 %copy-start.49 = (f32[32]{0:T(128)}, f32[32]{0:T(128)S(1)}, u32[]{:S(2)}) copy-start(f32[32]{0:T(128)S(1)} %multiply_power_fusion) | copy-start | bytes 388
  13.0 53.2 %copy-start.23 = (f32[1024,32]{0,1:T(8,128)}, f32[1024,32]{0,1:T(8,128)S(1)}, u32[]{:S(2)}) copy-start(f32[1024,32]{0,1:T(8,128)S(1)} %get-tuple-element.368) | copy-start | bytes 393220
  13.0 53.2 %copy-start.25 = (f32[1024,32]{0,1:T(8,128)}, f32[1024,32]{0,1:T(8,128)S(1)}, u32[]{:S(2)}) copy-start(f32[1024,32]{0,1:T(8,128)S(1)} %get-tuple-element.369) | copy-start | bytes 393220
  15.5 50.2 %copy-start.17 = (bf16[2048,64]{1,0:T(8,128)(2,1)}, bf16[2048,64]{1,0:T(8,128)(2,1)S(1)}, u32[]{:S(2)}) copy-start(bf16[2048,64]{1,0:T(8,128)(2,1)S(1)} %get-tuple-element.370) | copy-start | bytes 786436
  95.9 6.4 copy-start.10
  102.4 88.5 %copy-start.7 = (bf16[128,2048]{1,0:T(8,128)(2,1)S(1)}, bf16[128,2048]{1,0:T(8,128)(2,1)}, u32[]{:S(2)}) copy-start(bf16[128,2048]{1,0:T(8,128)(2,1)} %param.19) | copy-start | bytes 1572868
  102.4 90.5 %copy-start.36 = (f32[2048]{0:T(1024)S(1)}, f32[2048]{0:T(1024)}, u32[]{:S(2)}) copy-start(f32[2048]{0:T(1024)} %param.30) | copy-start | bytes 24580
  102.4 137.3 %all-gather.7.cloned.1.call-start = ((), (), s32[]{:S(2)}) async-start(), calls=%async_computation.6 | async-start | bytes 4718592 | tf_op jit(solution)/shard_map/all_gather | solution.py:142
  192.9 213.3 %copy-start.3 = (f32[128,2048]{1,0:T(8,128)}, f32[128,2048]{1,0:T(8,128)S(1)}, u32[]{:S(2)}) copy-start(f32[128,2048]{1,0:T(8,128)S(1)} %get-tuple-element.340) | copy-start | bytes 3145732
  192.9 213.3 %copy-start.45 = (f32[128]{0:T(128)}, f32[128]{0:T(128)S(1)}, u32[]{:S(2)}) copy-start(f32[128]{0:T(128)S(1)} %add_rsqrt_fusion.2) | copy-start | bytes 1540
  194.1 93.2 %all-gather.9.cloned.1.call-start = ((), (), s32[]{:S(2)}) async-start(), calls=%async_computation.8 | async-start | bytes 4718592 | tf_op jit(solution)/shard_map/all_gather | solution.py:162
  194.6 209.4 %reduce-scatter.9.cloned.1.call-start = ((), (), s32[]{:S(2)}) async-start(), calls=%async_computation.9 | async-start | bytes 9437184 | tf_op jit(solution)/shard_map/reduce_scatter | solution.py:169
  315.7 90.5 %copy-start.12 = (bf16[128,2048]{1,0:T(8,128)(2,1)S(1)}, bf16[128,2048]{1,0:T(8,128)(2,1)}, u32[]{:S(2)}) copy-start(bf16[128,2048]{1,0:T(8,128)(2,1)} %param.33) | copy-start | bytes 1572868
  315.7 93.0 %copy-start.51 = (f32[64]{0:T(128)S(1)}, f32[64]{0:T(128)}, u32[]{:S(2)}) copy-start(f32[64]{0:T(128)} %param.31) | copy-start | bytes 772
  315.7 138.5 %all-gather.11.cloned.1.call-start = ((), (), s32[]{:S(2)}) async-start(), calls=%async_computation.10 | async-start | bytes 4718592 | tf_op jit(solution)/shard_map/all_gather | solution.py:174
  408.6 235.2 %reduce-scatter.11.cloned.1.call-start = ((), (), s32[]{:S(2)}) async-start(), calls=%async_computation.11 | async-start | bytes 9437184 | tf_op jit(solution)/shard_map/reduce_scatter | solution.py:225
  409.3 50.1 %copy-start.58 = (s32[2]{0:T(128)S(1)}, s32[2]{0:T(128)}, u32[]{:S(2)}) copy-start(s32[2]{0:T(128)} %get-tuple-element.654) | copy-start | bytes 28
  459.4 83.9 %copy-start.6 = (f32[1024,384]{0,1:T(8,128)S(1)}, f32[1024,384]{0,1:T(8,128)}, u32[]{:S(2)}) copy-start(f32[1024,384]{0,1:T(8,128)} %copy-done.5) | copy-start | bytes 4718596
  459.4 8.6 copy-start.11
  480.8 6.7 copy-start.2
  499.8 8.5 copy-start.11
  521.1 6.7 copy-start.2
  540.3 7.3 copy-start.24
  540.3 7.3 copy-start.26
  540.3 7.5 copy-start.33
  540.4 7.5 copy-start.52
  555.3 140.8 %reduce-scatter.7.cloned.1.call-start = ((), (), s32[]{:S(2)}) async-start(), calls=%async_computation.7 | async-start | bytes 4718592 | tf_op jit(solution)/shard_map/reduce_scatter | solution.py:149
  564.7 649.7 %all-reduce.8.cloned.1.call-start = ((), (), s32[]{:S(2)}) async-start(), calls=%async_computation.13 | async-start | bytes 58720256 | tf_op jit(solution)/shard_map/psum | solution.py:242
  565.1 10.9 copy-start.60
  602.9 797.7 %all-reduce.6.cloned.1.call-start = ((), (), s32[]{:S(2)}) async-start(), calls=%async_computation.12 | async-start | bytes 16777216 | tf_op jit(solution)/shard_map/psum | solution.py:243
  621.9 21.9 %copy-start.8 = (bf16[128,2048]{1,0:T(8,128)(2,1)S(1)}, bf16[128,2048]{1,0:T(8,128)(2,1)}, u32[]{:S(2)}) copy-start(bf16[128,2048]{1,0:T(8,128)(2,1)} %param.19) | copy-start | bytes 1572868
  621.9 21.9 %copy-start.41 = (f32[2048]{0:T(1024)S(1)}, f32[2048]{0:T(1024)}, u32[]{:S(2)}) copy-start(f32[2048]{0:T(1024)} %param.29) | copy-start | bytes 24580
  621.9 21.9 %copy-start.48 = (f32[128]{0:T(128)S(1)}, f32[128]{0:T(128)}, u32[]{:S(2)}) copy-start(f32[128]{0:T(128)} %copy-done.47) | copy-start | bytes 1540
  621.9 24.2 %copy-start.44 = (f32[2048]{0:T(1024)S(1)}, f32[2048]{0:T(1024)}, u32[]{:S(2)}) copy-start(f32[2048]{0:T(1024)} %get-tuple-element.282) | copy-start | bytes 24580
  621.9 24.1 %copy-start.55 = (f32[64]{0:T(128)S(1)}, f32[64]{0:T(128)}, u32[]{:S(2)}) copy-start(f32[64]{0:T(128)} %get-tuple-element.284) | copy-start | bytes 772
  621.9 74.1 %copy-start.4 = (f32[128,2048]{1,0:T(8,128)S(1)}, f32[128,2048]{1,0:T(8,128)}, u32[]{:S(2)}) copy-start(f32[128,2048]{1,0:T(8,128)} %copy-done.3) | copy-start | bytes 3145732
  621.9 74.1 %copy-start.9 = (f32[128,2048]{1,0:T(8,128)S(1)}, f32[128,2048]{1,0:T(8,128)}, u32[]{:S(2)}) copy-start(f32[128,2048]{1,0:T(8,128)} %reduce-scatter.9.cloned.1.call-done) | copy-start | bytes 3145732
  621.9 74.1 %copy-start.13 = (bf16[128,2048]{1,0:T(8,128)(2,1)S(1)}, bf16[128,2048]{1,0:T(8,128)(2,1)}, u32[]{:S(2)}) copy-start(bf16[128,2048]{1,0:T(8,128)(2,1)} %param.33) | copy-start | bytes 1572868
  621.9 74.1 %copy-start.37 = (f32[2048]{0:T(1024)S(1)}, f32[2048]{0:T(1024)}, u32[]{:S(2)}) copy-start(f32[2048]{0:T(1024)} %param.30) | copy-start | bytes 24580
  621.9 74.1 %copy-start.46 = (f32[128]{0:T(128)S(1)}, f32[128]{0:T(128)}, u32[]{:S(2)}) copy-start(f32[128]{0:T(128)} %copy-done.45) | copy-start | bytes 1540
  622.0 74.1 %copy-start.54 = (f32[128]{0:T(128)S(1)}, f32[128]{0:T(128)}, u32[]{:S(2)}) copy-start(f32[128]{0:T(128)} %copy-done.53) | copy-start | bytes 1540
  1408.6 10.5 slice-start.4
  1409.9 9.1 slice-start.5
  1409.9 13.4 slice-start.2
  (41 other events, 121.6 us)
Sparse Core Ops, SparseCore 0:
  11.3 49.8 all-gather.4
  102.5 88.3 reduce-scatter.4
  194.2 45.4 all-gather.6
  241.2 46.0 all-gather.8
  315.8 88.1 reduce-scatter.8
  408.7 45.4 all-gather.10
  555.4 88.3 reduce-scatter.10
  646.6 49.3 reduce-scatter.6
  700.9 513.4 all-reduce.7
  1221.7 178.9 all-reduce.5
where the time goes:
time: 1450 us; the launch traced here: 1440 us
  waiting for transfers between devices  1070 us (74%)
  matrix products  149 us (10%)
  local copies, waits for them, and re-layouts  107 us (7%)
  other arithmetic  46.2 us (3%)
  blocking collectives  40 us (3%)
  between operations  17 us (1%)
    psum x1, waiting for transfers between devices, per_device(): lax.psum((grad_w_query, grad_w_output, grad_w_gate, grad_w_up, grad_w_dow...  515 us
    psum x1, waiting for transfers between devices, per_device(): lax.psum((grad_w_key, grad_w_value, grad_attn_gain, grad_ffn_gain, grad_q...  183 us
    reduce_scatter x1, waiting for transfers between devices, per_device(): lax.psum_scatter(matmul_right_t(grad_gate_up, w_ffn), 'mp', scatter_dimen...  88.1 us
    reduce_scatter x1, waiting for transfers between devices, per_device(): lax.psum_scatter(matmul(context, w_output), 'mp', scatter_dimension=0, ti...  88 us
    all_gather x1, waiting for transfers between devices, per_device(): gathered_one = lax.all_gather(h_one, 'mp', axis=0, tiled=True)  45.7 us
    all_gather x1, waiting for transfers between devices, per_device(): lax.all_gather(grad_mid.astype(jnp.bfloat16), 'mp', axis=0, tiled=True)  44.9 us
    psum x1, blocking collectives, per_device(): lax.psum((grad_w_key, grad_w_value, grad_attn_gain, grad_ffn_gain, grad_q...  40 us
    unnamed x125, local copies, waits for them, and re-layouts  39.9 us
  transfers between devices with their start and end apart: 10, of which 10 were waited for; matrix products, arithmetic and copies ran while one was open for 7% of the time, Pallas kernels for 0%

commit v1 on v0

--- a/solution.py
+++ b/solution.py
@@ -241,8 +241,18 @@
     grad_w_up = grad_w_ffn[:, ffn_width:]
     summed = lax.psum((grad_w_query, grad_w_output, grad_w_gate, grad_w_up, grad_w_down), "dp")
     shared = lax.psum(
-        (grad_w_key, grad_w_value, grad_attn_gain, grad_ffn_gain, grad_query_gain, grad_key_gain),
-        ("dp", "mp"),
+        lax.psum(
+            (
+                grad_w_key,
+                grad_w_value,
+                grad_attn_gain,
+                grad_ffn_gain,
+                grad_query_gain,
+                grad_key_gain,
+            ),
+            "mp",
+        ),
+        "dp",
     )
     entry_count = tok_count * model_width * lax.axis_size("dp") * lax.axis_size("mp")
     residual_rms = jnp.sqrt(squares_total / entry_count).reshape(1)

time: 1450 us -> 1570 us (1.083)
  waiting for transfers between devices: 1070 us -> 1180 us
  blocking collectives: 40 us -> 84.6 us
  matrix products: 149 us -> 126 us
    psum x1, waiting for transfers between devices: 515 us -> 623 us  [per_device(): lax.psum((grad_w_query, grad_w_output, grad_w_gate, grad_w_up, grad_w_dow...]
    reduce_scatter x1, waiting for transfers between devices: 21.1 us -> 91.9 us  [per_device(): lax.psum_scatter(matmul_right_t(grad_proj, w_attn), 'mp', scatter_dimensi...]
    psum x1, waiting for transfers between devices: 183 us -> 123 us  [per_device(): lax.psum((grad_w_key, grad_w_value, grad_attn_gain, grad_ffn_gain, grad_q...]
    psum x0 -> x2, blocking collectives: none -> 56.9 us  [the longest x1 39.9 us: per_device(): squares_total = lax.psum(squares_local, ('dp', 'mp'))]
    unnamed x125 -> x141, local copies, waits for them, and re-layouts: 39.9 us -> 43.7 us
  transfers between devices with their start and end apart: 10 -> 10, of which waited for: 10 -> 9; matrix products, arithmetic and copies ran while one was open for 7% -> 5% of each run, Pallas kernels for 0% -> 0%
where the time goes in v1:
time: 1570 us; the launch traced here: 1560 us
  waiting for transfers between devices  1180 us (75%)
  matrix products  126 us (8%)
  local copies, waits for them, and re-layouts  104 us (7%)
  blocking collectives  84.6 us (5%)
  other arithmetic  38.4 us (2%)
  between operations  17.1 us (1%)
    psum x1, waiting for transfers between devices, per_device(): lax.psum((grad_w_query, grad_w_output, grad_w_gate, grad_w_up, grad_w_dow...  623 us
    psum x1, waiting for transfers between devices, per_device(): lax.psum((grad_w_key, grad_w_value, grad_attn_gain, grad_ffn_gain, grad_q...  123 us
    reduce_scatter x1, waiting for transfers between devices, per_device(): lax.psum_scatter(matmul_right_t(grad_proj, w_attn), 'mp', scatter_dimensi...  91.9 us
    reduce_scatter x1, waiting for transfers between devices, per_device(): lax.psum_scatter(matmul(context, w_output), 'mp', scatter_dimension=0, ti...  88.4 us
    reduce_scatter x1, waiting for transfers between devices, per_device(): lax.psum_scatter(matmul_right_t(grad_gate_up, w_ffn), 'mp', scatter_dimen...  88.4 us
    all_gather x1, waiting for transfers between devices, per_device(): gathered_one = lax.all_gather(h_one, 'mp', axis=0, tiled=True)  46.9 us
    all_gather x1, waiting for transfers between devices, per_device(): lax.all_gather(grad_mid.astype(jnp.bfloat16), 'mp', axis=0, tiled=True)  45.3 us
    unnamed x141, local copies, waits for them, and re-layouts  43.7 us
  transfers between devices with their start and end apart: 10, of which 9 were waited for; matrix products, arithmetic and copies ran while one was open for 5% of the time, Pallas kernels for 0%

profile of v1, /device:TPU:0, one launch (start us, length us, event | category | flops | bytes accessed | tf_op | source)
XLA Modules:
  0.0 1557.0 jit_solution(9329483233171797584)
XLA Ops:
  14.3 46.9 %all-gather.5.cloned.1.call-done = bf16[1024,2048]{1,0:T(8,128)(2,1)} async-done(((bf16[128,2048]{1,0:T(8,128)(2,1)}), bf16[1024,2048]{1,0:T(8,128)(2,1)}) %all-gather.5.cloned.1.call-update) | async-done | bytes 4194320 | tf_op jit(solution)/shard_map/all_gather | solution.py:92
  61.2 4.0 fusion.78
  68.0 23.7 %while.28 = (s32[]{:T(128)}, bf16[2,512,4,64]{1,3,2,0:T(8,128)(2,1)}, f32[2,4,512]{2,1,0:T(4,128)S(1)}, s32[2]{0:T(128)S(1)}, s32[1024]{0:T(1024)S(1)}, /*index=...) while((s32[]{:T(128)}, ...), condition=%wide.region_6.7_spmd.clone, body=%wide.region_3.6_spmd.clone.sunk | while | flops 563739136 | bytes 32323824 | solution.py:134
  73.5 2.4 fusion.147
  76.0 3.1 fusion.148
  85.4 2.4 fusion.147
  87.8 3.1 fusion.148
  93.4 4.7 fusion.102
  98.2 88.4 %reduce-scatter.5.cloned.1.call-done = f32[128,2048]{1,0:T(8,128)} async-done(((f32[1024,2048]{1,0:T(8,128)}), f32[128,2048]{1,0:T(8,128)}) %reduce-scatter.5.cloned.1.call-update) | async-done | bytes 1048592 | tf_op jit(solution)/shard_map/reduce_scatter | solution.py:136
  190.4 4.8 constant_dynamic-update-slice_fusion.1
  195.2 2.5 constant_dynamic-update-slice_fusion
  197.7 37.7 %all-gather.7.cloned.1.call-done = bf16[1024,2048]{1,0:T(8,128)(2,1)} async-done(((bf16[128,2048]{1,0:T(8,128)(2,1)}), bf16[1024,2048]{1,0:T(8,128)(2,1)}) %all-gather.7.cloned.1.call-update) | async-done | bytes 4194320 | tf_op jit(solution)/shard_map/all_gather | solution.py:142
  235.4 14.9 fusion.103
  250.4 32.4 %all-gather.9.cloned.1.call-done = bf16[1024,2048]{1,0:T(8,128)(2,1)} async-done(((bf16[128,2048]{1,0:T(8,128)(2,1)}), bf16[1024,2048]{1,0:T(8,128)(2,1)}) %all-gather.9.cloned.1.call-update) | async-done | bytes 4194320 | tf_op jit(solution)/shard_map/all_gather | solution.py:162
  282.8 13.1 multiply_convert_fusion.1
  297.9 13.3 fusion.58
  311.3 88.4 %reduce-scatter.9.cloned.1.call-done = f32[128,2048]{1,0:T(8,128)} async-done(((f32[1024,2048]{1,0:T(8,128)}), f32[128,2048]{1,0:T(8,128)}) %reduce-scatter.9.cloned.1.call-update) | async-done | bytes 1048592 | tf_op jit(solution)/shard_map/reduce_scatter | solution.py:169
  404.6 45.3 %all-gather.11.cloned.1.call-done = bf16[1024,2048]{1,0:T(8,128)(2,1)} async-done(((bf16[128,2048]{1,0:T(8,128)(2,1)}), bf16[1024,2048]{1,0:T(8,128)(2,1)}) %all-gather.11.cloned.1.call-update) | async-done | bytes 4194320 | tf_op jit(solution)/shard_map/all_gather | solution.py:174
  449.9 3.5 convolution_convert_fusion.1
  454.4 54.9 %while.29 = (s32[]{:T(128)}, f32[1024,64]{0,1:T(8,128)S(1)}, f32[1024,64]{0,1:T(8,128)}, f32[2,512,4,64]{1,0,3,2:T(2,128)}, s32[2]{0:T(128)S(1)}, /*index=5*/s32...) while((s32[]{:T(128)}, f32[1024,64]{0,1:T(8,128)S(1)}, ...), condition=%wide.region_14.15_spmd.clone, body=%wide.region_12.14_spmd.clone.sunk | while | flops 1375664640 | bytes 70195432 | solution.py:209
  459.6 3.2 fusion.162
  462.7 2.9 fusion.159
  470.9 10.4 dynamic_update_slice.30
  486.5 4.1 fusion.162
  490.6 2.9 fusion.159
  498.8 10.4 dynamic_update_slice.30
  519.6 2.6 broadcast_in_dim.64.clone.1
  522.1 5.9 dynamic_update_slice.19
  528.1 2.5 broadcast_in_dim.64.clone
  530.6 5.8 dynamic_update_slice.18
  538.1 6.0 fusion.77
  545.8 8.2 convolution_convert_fusion
  554.4 10.9 fusion.105
  565.3 11.1 fusion.57
  576.4 6.8 fusion.100
  584.7 4.8 fusion.104
  589.5 123.0 %all-reduce.7.cloned.1.call-done = (f32[2048,512]{1,0:T(8,128)}, f32[2048,512]{1,0:T(8,128)}) async-done(((f32[2048,512]{1,0:T(8,128)}, f32[2048,512]{1,0:T(8,128)}), (f32[2048,512]{1,0:T(8,128)}, f32[2048,512]{1,0:T(8,128)})) %all-reduce.7.cloned.1.call-update) | async-done | bytes 8388624 | tf_op jit(solution)/shard_map/psum | solution.py:244
  713.3 91.9 %reduce-scatter.11.cloned.1.call-done = f32[128,2048]{1,0:T(8,128)} async-done(((f32[1024,2048]{1,0:T(8,128)}), f32[128,2048]{1,0:T(8,128)}) %reduce-scatter.11.cloned.1.call-update) | async-done | bytes 1048592 | tf_op jit(solution)/shard_map/reduce_scatter | solution.py:225
  807.4 39.9 %psum.143 = f32[]{:T(128)} all-reduce(f32[]{:T(128)} %get-tuple-element.288), channel_id=1, replica_groups=mesh['dp'=4,'mp'=8] {'dp','mp'}, use_global_device_ids=true, to_apply=%region_42.43 | all-reduce | flops 1 | bytes 8 | tf_op jit(solution)/shard_map/psum | solution.py:160
  848.0 27.7 %all-reduce = (f32[2048]{0:T(1024)S(1)}, f32[2048]{0:T(1024)S(1)}, f32[64]{0:T(128)S(1)}, f32[64]{0:T(128)S(1)}) all-reduce(f32[2048]{0:T(1024)S(1)} %get-tuple-element.286, f32[2048]{0:T(1024)S(1)} %copy-done.44, f32[64]{0:T(128)S(1)} %reduce_sum.172, f32[64]{0:T(128)S(1)} %get-tuple-element.284), channel_id=1, replica_groups=mesh['dp'=4,'mp'=8] {'mp'}, use_global_device_ids=true, to_apply=%region_29.30 | all-reduce | flops 4224 | bytes 33792 | tf_op jit(solution)/shard_map/psum | solution.py:244
  875.7 17.0 %all-reduce.2 = (f32[2048]{0:T(1024)}, f32[2048]{0:T(1024)}, f32[64]{0:T(128)}, f32[64]{0:T(128)}) all-reduce(f32[2048]{0:T(1024)S(1)} %get-tuple-element.327, f32[2048]{0:T(1024)S(1)} %get-tuple-element.328, f32[64]{0:T(128)S(1)} %get-tuple-element.329, f32[64]{0:T(128)S(1)} %get-tuple-element.330), channel_id=1, replica_groups=mesh['dp'=4,'mp'=8] {'dp'}, use_global_device_ids=true, to_apply=%region_30.31 | all-reduce | flops 4224 | bytes 33792 | tf_op jit(solution)/shard_map/psum | solution.py:243
  892.7 3.1 fusion.72
  896.4 622.6 %all-reduce.9.cloned.1.call-done = (f32[2048,256]{0,1:T(8,128)}, f32[2048,512]{1,0:T(8,128)}, f32[2048,512]{1,0:T(8,128)}, f32[256,2048]{1,0:T(8,128)}, f32[2048...) async-done(((f32[2048,256]{0,1:T(8,128)}, f32[2048,512]{1,0:T(8,128)}, f32[2048,512]{1,0:T(8,128)}, f32[256,2048]{1,0:T(8,128)}, f32[2048,1024]{1,0:T(8,128)}, ...) | async-done | bytes 37748752 | tf_op jit(solution)/shard_map/psum | solution.py:242
  1518.9 2.9 copy.57
  1521.8 4.8 copy.119
  1531.1 9.1 copy.122
  1540.2 4.3 copy.123
  1545.4 3.4 copy.124
  (256 shorter events, 72.6 us)
Async XLA Ops:
  7.2 86.2 %copy-start = (bf16[256,2048]{1,0:T(8,128)(2,1)S(1)}, bf16[256,2048]{1,0:T(8,128)(2,1)}, u32[]{:S(2)}) copy-start(bf16[256,2048]{1,0:T(8,128)(2,1)} %param.25) | copy-start | bytes 3145732
  7.2 54.0 %copy-start.26 = (bf16[2048,256]{1,0:T(8,128)(2,1)S(1)}, bf16[2048,256]{1,0:T(8,128)(2,1)}, u32[]{:S(2)}) copy-start(bf16[2048,256]{1,0:T(8,128)(2,1)} %param.22) | copy-start | bytes 3145732
  7.2 54.0 %all-gather.5.cloned.1.call-start = ((), (), s32[]{:S(2)}) async-start(), calls=%async_computation.4 | async-start | bytes 4718592 | tf_op jit(solution)/shard_map/all_gather | solution.py:92
  11.2 175.4 %reduce-scatter.5.cloned.1.call-start = ((), (), s32[]{:S(2)}) async-start(), calls=%async_computation.5 | async-start | bytes 9437184 | tf_op jit(solution)/shard_map/reduce_scatter | solution.py:136
  12.0 53.7 %copy-start.40 = (f32[1024]{0:T(1024)}, f32[1024]{0:T(1024)S(1)}, u32[]{:S(2)}) copy-start(f32[1024]{0:T(1024)S(1)} %convert_element_type.62) | copy-start | bytes 12292
  12.0 53.7 %copy-start.49 = (f32[32]{0:T(128)}, f32[32]{0:T(128)S(1)}, u32[]{:S(2)}) copy-start(f32[32]{0:T(128)S(1)} %multiply_power_fusion) | copy-start | bytes 388
  12.6 54.1 %copy-start.24 = (f32[1024,32]{0,1:T(8,128)}, f32[1024,32]{0,1:T(8,128)S(1)}, u32[]{:S(2)}) copy-start(f32[1024,32]{0,1:T(8,128)S(1)} %get-tuple-element.373) | copy-start | bytes 393220
  12.6 54.1 %copy-start.25 = (f32[1024,32]{0,1:T(8,128)}, f32[1024,32]{0,1:T(8,128)S(1)}, u32[]{:S(2)}) copy-start(f32[1024,32]{0,1:T(8,128)S(1)} %get-tuple-element.374) | copy-start | bytes 393220
  14.2 51.0 %copy-start.15 = (bf16[2048,64]{1,0:T(8,128)(2,1)}, bf16[2048,64]{1,0:T(8,128)(2,1)S(1)}, u32[]{:S(2)}) copy-start(bf16[2048,64]{1,0:T(8,128)(2,1)S(1)} %get-tuple-element.375) | copy-start | bytes 786436
  14.3 51.0 %copy-start.17 = (bf16[2048,64]{1,0:T(8,128)(2,1)}, bf16[2048,64]{1,0:T(8,128)(2,1)S(1)}, u32[]{:S(2)}) copy-start(bf16[2048,64]{1,0:T(8,128)(2,1)S(1)} %get-tuple-element.376) | copy-start | bytes 786436
  61.2 4.3 copy-start.51
  61.2 5.2 copy-start.53
  93.4 4.7 copy-start.19
  98.1 88.5 %copy-start.6 = (bf16[128,2048]{1,0:T(8,128)(2,1)S(1)}, bf16[128,2048]{1,0:T(8,128)(2,1)}, u32[]{:S(2)}) copy-start(bf16[128,2048]{1,0:T(8,128)(2,1)} %param.19) | copy-start | bytes 1572868
  98.1 90.5 %copy-start.37 = (f32[2048]{0:T(1024)S(1)}, f32[2048]{0:T(1024)}, u32[]{:S(2)}) copy-start(f32[2048]{0:T(1024)} %param.30) | copy-start | bytes 24580
  98.1 137.3 %all-gather.7.cloned.1.call-start = ((), (), s32[]{:S(2)}) async-start(), calls=%async_computation.6 | async-start | bytes 4718592 | tf_op jit(solution)/shard_map/all_gather | solution.py:142
  188.6 213.2 %copy-start.2 = (f32[128,2048]{1,0:T(8,128)}, f32[128,2048]{1,0:T(8,128)S(1)}, u32[]{:S(2)}) copy-start(f32[128,2048]{1,0:T(8,128)S(1)} %get-tuple-element.345) | copy-start | bytes 3145732
  188.6 213.2 %copy-start.45 = (f32[128]{0:T(128)}, f32[128]{0:T(128)S(1)}, u32[]{:S(2)}) copy-start(f32[128]{0:T(128)S(1)} %add_rsqrt_fusion.2) | copy-start | bytes 1540
  189.8 93.0 %all-gather.9.cloned.1.call-start = ((), (), s32[]{:S(2)}) async-start(), calls=%async_computation.8 | async-start | bytes 4718592 | tf_op jit(solution)/shard_map/all_gather | solution.py:162
  190.4 209.3 %reduce-scatter.9.cloned.1.call-start = ((), (), s32[]{:S(2)}) async-start(), calls=%async_computation.9 | async-start | bytes 9437184 | tf_op jit(solution)/shard_map/reduce_scatter | solution.py:169
  190.4 4.8 copy-start.11
  311.2 90.6 %copy-start.9 = (bf16[128,2048]{1,0:T(8,128)(2,1)S(1)}, bf16[128,2048]{1,0:T(8,128)(2,1)}, u32[]{:S(2)}) copy-start(bf16[128,2048]{1,0:T(8,128)(2,1)} %param.33) | copy-start | bytes 1572868
  311.2 93.2 %copy-start.54 = (f32[64]{0:T(128)S(1)}, f32[64]{0:T(128)}, u32[]{:S(2)}) copy-start(f32[64]{0:T(128)} %param.31) | copy-start | bytes 772
  311.3 138.6 %all-gather.11.cloned.1.call-start = ((), (), s32[]{:S(2)}) async-start(), calls=%async_computation.10 | async-start | bytes 4718592 | tf_op jit(solution)/shard_map/all_gather | solution.py:174
  401.8 51.5 %copy-start.55 = (f32[128]{0:T(128)}, f32[128]{0:T(128)S(1)}, u32[]{:S(2)}) copy-start(f32[128]{0:T(128)S(1)} %broadcast_multiply_fusion.3) | copy-start | bytes 1540
  404.2 308.3 %all-reduce.7.cloned.1.call-start = ((), (), s32[]{:S(2)}) async-start(), calls=%async_computation.12 | async-start | bytes 16777216 | tf_op jit(solution)/shard_map/psum | solution.py:244
  509.4 4.0 copy-start.5
  509.4 4.3 copy-start.36
  536.5 268.6 %reduce-scatter.11.cloned.1.call-start = ((), (), s32[]{:S(2)}) async-start(), calls=%async_computation.11 | async-start | bytes 9437184 | tf_op jit(solution)/shard_map/reduce_scatter | solution.py:225
  544.2 348.5 %reduce-scatter.7.cloned.1.call-start = ((), (), s32[]{:S(2)}) async-start(), calls=%async_computation.7 | async-start | bytes 4718592 | tf_op jit(solution)/shard_map/reduce_scatter | solution.py:149
  554.0 965.0 %all-reduce.9.cloned.1.call-start = ((), (), s32[]{:S(2)}) async-start(), calls=%async_computation.13 | async-start | bytes 75497472 | tf_op jit(solution)/shard_map/psum | solution.py:242
  554.4 10.9 copy-start.59
  576.4 6.8 copy-start.14
  712.5 92.6 %copy-start.7 = (bf16[128,2048]{1,0:T(8,128)(2,1)S(1)}, bf16[128,2048]{1,0:T(8,128)(2,1)}, u32[]{:S(2)}) copy-start(bf16[128,2048]{1,0:T(8,128)(2,1)} %param.19) | copy-start | bytes 1572868
  712.5 92.6 %copy-start.39 = (f32[2048]{0:T(1024)S(1)}, f32[2048]{0:T(1024)}, u32[]{:S(2)}) copy-start(f32[2048]{0:T(1024)} %param.29) | copy-start | bytes 24580
  712.5 92.6 %copy-start.48 = (f32[128]{0:T(128)S(1)}, f32[128]{0:T(128)}, u32[]{:S(2)}) copy-start(f32[128]{0:T(128)} %copy-done.47) | copy-start | bytes 1540
  712.5 135.5 %copy-start.44 = (f32[2048]{0:T(1024)S(1)}, f32[2048]{0:T(1024)}, u32[]{:S(2)}) copy-start(f32[2048]{0:T(1024)} %get-tuple-element.282) | copy-start | bytes 24580
  712.5 180.2 %copy-start.3 = (f32[128,2048]{1,0:T(8,128)S(1)}, f32[128,2048]{1,0:T(8,128)}, u32[]{:S(2)}) copy-start(f32[128,2048]{1,0:T(8,128)} %copy-done.2) | copy-start | bytes 3145732
  712.5 180.2 %copy-start.8 = (f32[128,2048]{1,0:T(8,128)S(1)}, f32[128,2048]{1,0:T(8,128)}, u32[]{:S(2)}) copy-start(f32[128,2048]{1,0:T(8,128)} %reduce-scatter.9.cloned.1.call-done) | copy-start | bytes 3145732
  712.5 180.2 %copy-start.10 = (bf16[128,2048]{1,0:T(8,128)(2,1)S(1)}, bf16[128,2048]{1,0:T(8,128)(2,1)}, u32[]{:S(2)}) copy-start(bf16[128,2048]{1,0:T(8,128)(2,1)} %param.33) | copy-start | bytes 1572868
  712.5 180.2 %copy-start.38 = (f32[2048]{0:T(1024)S(1)}, f32[2048]{0:T(1024)}, u32[]{:S(2)}) copy-start(f32[2048]{0:T(1024)} %param.30) | copy-start | bytes 24580
  712.6 180.2 %copy-start.46 = (f32[128]{0:T(128)S(1)}, f32[128]{0:T(128)}, u32[]{:S(2)}) copy-start(f32[128]{0:T(128)} %copy-done.45) | copy-start | bytes 1540
  712.6 180.2 %copy-start.56 = (f32[128]{0:T(128)S(1)}, f32[128]{0:T(128)}, u32[]{:S(2)}) copy-start(f32[128]{0:T(128)} %copy-done.55) | copy-start | bytes 1540
  1521.8 4.8 copy-start.12
  1529.8 10.5 slice-start.2
  1531.1 9.1 slice-start.3
  1531.1 13.4 slice-start
  1540.2 5.2 slice-start.1
  (31 other events, 63.3 us)
Sparse Core Ops, SparseCore 0:
  11.3 49.8 all-gather.4
  98.2 88.3 reduce-scatter.4
  189.9 45.4 all-gather.6
  236.9 45.8 all-gather.8
  311.4 88.2 reduce-scatter.8
  404.3 45.4 all-gather.10
  536.6 175.8 all-reduce.6
  715.4 89.7 reduce-scatter.10
  808.0 49.4 reduce-scatter.6
  862.7 656.2 all-reduce.8
